TPU v7x, 32 devices: a whole 2x2x4 slice. The times are simulated.
32 devices in a mesh: pop: 2 (over x), dp: 8 (over z, y), tp: 2 (over core).
Axes of the slice: x: 2, y: 2, z: 4, core: 2. Of those that a mesh axis runs over, the one named last changes fastest.
Arguments:
- q_latent: bfloat16 [256, 128, 512], P(('pop', 'dp')), parts along dimension 0
- q_rope: bfloat16 [256, 8192], P(('pop', 'dp')), parts along dimension 0
- new_entry: bfloat16 [256, 576], P(('pop', 'dp')), parts along dimension 0
- cache_latent: bfloat16 [768, 64, 512], P(('pop', 'dp'), 'tp'), parts along dimension 0, may hold values from -6 to 6
- cache_rope: bfloat16 [768, 4096], P(('pop', 'dp'), 'tp'), parts along dimension 0, may hold values from -6 to 6
- source_rank: int32 [256, 16, 1], P(('pop', 'dp')), parts along dimension 0, may hold values from 0 to 7; in each aligned block of 256 rows (0 to 255, 256 to 511, ..., all dimensions but the last counted through in order) at most 40 rows name the same one
- slot_index: int32 [256, 16], P(('pop', 'dp')), parts along dimension 0, may hold values from 0 to 47
- lengths: int32 [256], P(('pop', 'dp')), parts along dimension 0, may hold values from 897 to 1024, as said below
- value_up_weight: bfloat16 [128, 512, 128], P('tp'), may hold values from -0.25 to 0.25
Outputs:
- attn_out: bfloat16 [256, 16384], P(('pop', 'dp'), 'tp'), parts along dimension 0
There are 2 independent parts, one for each index of `pop`. A program takes and returns all parts, laid end to end along the dimension named above; an argument that names none is the same for every part. Nothing has to cross between parts.
Inputs may be any that keep to these rules, and one draw needn't show every extreme that they name: `source_rank`: within the table rows of the 16 requests of one dp rank, no source rank is named more than 40 times; in some ranks' rows one source rank is named exactly 40 times. `lengths`: some request has the full length 1024.
All inputs are finite; a program needn't handle non-finite values.
Results may differ from a plain program's by a relative error of at most 0.0052.
Values may be sent and summed in bfloat16 or wider, within the bound.
A program may use at most 128 MiB of HBM per device.

v0:
```python
import jax
import jax.numpy as jnp
from jax import lax
from jax.sharding import PartitionSpec as P

softmax_scale = 192.0 ** (-0.5)
neg_fill = -1e30


def entry_places(src_flat, rank_count):
    onehot = (src_flat[:, None] == jnp.arange(rank_count, dtype=jnp.int32)[None, :]).astype(
        jnp.int32
    )
    before = jnp.cumsum(onehot, axis=0) - onehot
    return jnp.sum(before * onehot, axis=1)


def local(
    q_latent,
    q_rope,
    new_entry,
    cache_latent,
    cache_rope,
    source_rank,
    slot_index,
    lengths,
    value_up_weight,
):
    rank_count = lax.axis_size("dp")
    lane_count = lax.axis_size("tp")
    my_lane = lax.axis_index("tp")
    requests, max_blocks = slot_index.shape
    run_len = cache_latent.shape[1]
    latent_dim = cache_latent.shape[2]
    heads = q_latent.shape[1]
    rope_dim = q_rope.shape[1] // heads
    entries = requests * max_blocks
    capacity = max(2, (entries * 5 + 4 * rank_count - 1) // (4 * rank_count))
    src_flat = source_rank.reshape(entries)
    slot_flat = slot_index.reshape(entries)
    places = entry_places(src_flat, rank_count)
    wanted = jnp.zeros((rank_count, capacity), jnp.int32).at[src_flat, places].set(slot_flat)
    asked_slots = lax.all_to_all(wanted, "dp", split_axis=0, concat_axis=0, tiled=True)
    send_latent = jnp.take(cache_latent, asked_slots, axis=0)
    send_rope = jnp.take(cache_rope, asked_slots, axis=0)
    got_latent, received_rotary_keys = (
        lax.all_to_all(send_latent, "dp", split_axis=0, concat_axis=0, tiled=True),
        lax.all_to_all(send_rope, "dp", split_axis=0, concat_axis=0, tiled=True),
    )
    where_from = src_flat * capacity + places
    keys_latent = jnp.take(
        got_latent.reshape(rank_count * capacity, run_len, latent_dim), where_from, axis=0
    )
    keys_latent = keys_latent.reshape(requests, max_blocks * run_len, latent_dim)
    keys_rope = jnp.take(
        received_rotary_keys.reshape(rank_count * capacity, run_len * rope_dim), where_from, axis=0
    )
    keys_rope = keys_rope.reshape(requests, max_blocks * run_len, rope_dim)
    query_rope = q_rope.reshape(requests, heads, rope_dim)
    scores = jnp.einsum("rhk,rnk->rhn", q_latent, keys_latent, preferred_element_type=jnp.float32)
    scores = (
        scores
        + jnp.einsum("rhd,rnd->rhn", query_rope, keys_rope, preferred_element_type=jnp.float32)
    ) * softmax_scale
    new_latent = new_entry[:, :latent_dim]
    incoming_rotary_key = new_entry[:, latent_dim:]
    new_score = jnp.einsum("rhk,rk->rh", q_latent, new_latent, preferred_element_type=jnp.float32)
    new_score = (
        new_score
        + jnp.einsum(
            "rhd,rd->rh", query_rope, incoming_rotary_key, preferred_element_type=jnp.float32
        )
    ) * softmax_scale
    slot_pos = jnp.arange(max_blocks * run_len, dtype=jnp.int32)
    positions = (
        slot_pos // run_len * (run_len * lane_count) + my_lane * run_len + slot_pos % run_len
    )
    in_range = (positions[None, :] < lengths[:, None])[:, None, :]
    is_first = my_lane == 0
    top_score = jnp.max(jnp.where(in_range, scores, neg_fill), axis=2)
    top_score = jnp.where(is_first, jnp.maximum(top_score, new_score), top_score)
    expo = jnp.where(in_range, jnp.exp(scores - top_score[:, :, None]), 0.0)
    numerator = jnp.einsum(
        "rhn,rnk->rhk", expo.astype(jnp.bfloat16), keys_latent, preferred_element_type=jnp.float32
    )
    denominator = jnp.sum(expo, axis=2)
    incoming_token_weight = jnp.where(is_first, jnp.exp(new_score - top_score), 0.0)
    numerator = (
        numerator
        + incoming_token_weight.astype(jnp.bfloat16).astype(jnp.float32)[:, :, None]
        * new_latent.astype(jnp.float32)[:, None, :]
    )
    denominator = denominator + incoming_token_weight
    overall = lax.pmax(top_score, "tp")
    factor = jnp.exp(top_score - overall)
    numer_sum, denom_sum = (
        lax.psum_scatter(numerator * factor[:, :, None], "tp", scatter_dimension=1, tiled=True),
        lax.psum_scatter(denominator * factor, "tp", scatter_dimension=1, tiled=True),
    )
    latent_output_rows = (numer_sum / denom_sum[:, :, None]).astype(jnp.bfloat16)
    value_projected_output = jnp.einsum(
        "wyc,yca->wya", latent_output_rows, value_up_weight, preferred_element_type=jnp.float32
    )
    return value_projected_output.reshape(requests, -1).astype(jnp.bfloat16)


def solution(mesh):
    placed = (
        P(("pop", "dp"), None, None),
        P(("pop", "dp"), None),
        P(("pop", "dp"), None),
        P(("pop", "dp"), "tp", None),
        P(("pop", "dp"), "tp"),
        P(("pop", "dp"), None, None),
        P(("pop", "dp"), None),
        P(("pop", "dp")),
        P("tp", None, None),
    )
    return jax.shard_map(
        local, mesh=mesh, in_specs=placed, out_specs=P(("pop", "dp"), "tp"), check_vma=False
    )
```

profile of v0, /device:TPU:0, one launch (start us, length us, event | category | flops | bytes accessed | tf_op | source)
XLA Modules:
  0.0 377.6 jit_solution(3026450740201988404)
XLA Ops:
  12.0 11.2 %scatter_fusion = s32[8,40]{1,0:T(8,128)S(1)} fusion(s32[8,40]{1,0:T(8,128)S(1)} %broadcast_in_dim.88, s32[256]{0:T(256)S(1)} %bitcast.59, s32[256]{0:T(256)S(1)} %reshape.251), kind=kCustom, calls=%fused_computation.4 | custom fusion | bytes 5120 | tf_op jit(solution)/shard_map/scatter | solution.py:42
  23.2 13.6 %all_to_all.25 = s32[8,1,40]{2,1,0:T(1,128)S(1)} all-to-all(s32[8,1,40]{2,1,0:T(1,128)S(1)} %bitcast.55), channel_id=1, replica_groups=mesh['pop'=2,'dp'=8,'tp'=2] {'dp'}, dimensions={0} | all-to-all | bytes 2560 | tf_op jit(solution)/shard_map/all_to_all | solution.py:43
  36.9 3.0 gather_fusion.2
  39.9 2.6 broadcast_select_fusion.1
  42.5 3.6 all-to-all-start.2
  46.1 12.0 %gather_fusion = bf16[320,32,512]{2,1,0:T(8,128)(2,1)} fusion(bf16[48,32,512]{2,1,0:T(8,128)(2,1)} %param.12, s32[1024]{0:T(1024)S(1)} %pad_clamp_fusion.1), kind=kCustom, calls=%fused_computation | custom fusion | bytes 20972800 | tf_op jit(solution)/shard_map/jit(_take)/gather | solution.py:44
  58.0 10.1 %broadcast_select_fusion = bf16[8,40,32,512]{3,2,1,0:T(8,128)(2,1)} fusion(bf16[8,40,32,512]{3,2,1,0:T(8,128)(2,1)} %bitcast.57, pred[8,40]{1,0:T(8,128)(4,1)S(1)} %compare_and_fusion.1), kind=kLoop, calls=%fused_computation.5 | loop fusion | flops 5242880 | bytes 20971840 | tf_op jit(solution)/shard_map/jit(_take)/select_n | solution.py:44
  68.2 8.3 %all-to-all-done.2 = bf16[8,40,2048]{2,1,0:T(8,128)(2,1)S(1)} async-done(((bf16[8,40,2048]{2,1,0:T(8,128)(2,1)}), bf16[8,40,2048]{2,1,0:T(8,128)(2,1)S(1)}, u32[]{:S(2)}, u32[]{:S(2)}) %all-to-all-start.2) | async-done | bytes 1310752 | tf_op jit(solution)/shard_map/all_to_all | solution.py:48
  76.4 5.2 %all-to-all-start.1 = ((bf16[8,40,32,512]{3,2,1,0:T(8,128)(2,1)}), bf16[8,40,32,512]{3,2,1,0:T(8,128)(2,1)}, u32[]{:S(2)}, u32[]{:S(2)}) async-start(bf16[8,40,32,512]{3,2,1,0:T(8,128)(2,1)} %broadcast_select_fusion), calls=%async_computation.1 | async-start | bytes 20971520 | tf_op jit(solution)/shard_map/all_to_all | solution.py:47
  82.1 2.3 reshape.216
  84.5 1.4 fusion.12
  86.6 2.4 gather_fusion.3
  89.0 4.4 %gather.25 = bf16[16,512,64]{2,1,0:T(8,128)(2,1)} reshape(bf16[256,2048]{1,0:T(8,128)(2,1)} %gather_fusion.3) | data formatting | bytes 2097152 | tf_op jit(solution)/shard_map/jit(_take)/gather | solution.py:55
  93.4 214.7 %all-to-all-done.1 = bf16[8,40,32,512]{3,2,1,0:T(8,128)(2,1)} async-done(((bf16[8,40,32,512]{3,2,1,0:T(8,128)(2,1)}), bf16[8,40,32,512]{3,2,1,0:T(8,128)(2,1)}, u32[]{:S(2)}, u32[]{:S(2)}) %all-to-all-start.1) | async-done | bytes 10485792 | tf_op jit(solution)/shard_map/all_to_all | solution.py:47
  308.1 12.6 %gather_fusion.1 = bf16[256,32,512]{2,1,0:T(8,128)(2,1)} fusion(bf16[320,32,512]{2,1,0:T(8,128)(2,1)} %bitcast.10, s32[1024]{0:T(1024)S(1)} %pad_clamp_fusion), kind=kCustom, calls=%fused_computation.1 | custom fusion | bytes 16778240 | tf_op jit(solution)/shard_map/jit(_take)/gather | solution.py:51
  320.7 4.7 %bitcast_select_fusion = bf16[16,512,512]{2,1,0:T(8,128)(2,1)S(1)} fusion(pred[16,512]{1,0:T(8,128)(4,1)S(1)} %broadcast_in_dim.86, bf16[16,512,512]{2,1,0:T(8,128)(2,1)} %bitcast.58), kind=kLoop, calls=%fused_computation.6 | loop fusion | flops 4194304 | bytes 16785408 | tf_op jit(solution)/shard_map/jit(_take)/select_n | solution.py:51
  325.4 2.3 fusion.28
  329.1 4.9 %select_reduce_fusion = (f32[16,128]{1,0:T(8,128)S(1)}, f32[16,512,128]{2,1,0:T(8,128)}) fusion(pred[16,512]{1,0:T(8,128)(4,1)S(1)} %broadcast_compare_fusion, f32[16,512,128]{2,1,0:T(8,128)S(1)} %fusion.28, bf16[16,128,64]{2,1,0:T(8,128)(2,1)S(1)} %copy-done.4, bf16[16,512,64]{2,1,0:T(8,128)(2,1)S(1)} %copy-done.3, pred[16,512]{1,0:T(8,128)(4,1)S(1)} %broadcast_in_dim.86), kind=kOutput, calls=%fused_computation.11 | convolution fusion | flops 138934272 | bytes 9723904 | tf_op jit(solution)/shard_map/rhd,rnd->rhn/dot_general | solution.py:63
  334.1 2.5 pmax.7
  336.5 3.6 bitcast_reduce_fusion
  341.0 7.6 %add_multiply_fusion = f32[16,128,512]{2,1,0:T(8,128)} fusion(bf16[16,512,512]{2,1,0:T(8,128)(2,1)} %copy-done.2, f32[16,512,128]{2,1,0:T(8,128)} %get-tuple-element.15, f32[16,128]{1,0:T(8,128)S(1)} %get-tuple-element.7, f32[16,512]{1,0:T(8,128)S(1)} %get-tuple-element.8, f32[16,128]{1,0:T(8,128)S(1)} %convert_element_type.52, ...), kind=kOutput, calls=%fused_computation.9 | convolution fusion | flops 1080033280 | bytes 16842752 | tf_op jit(solution)/shard_map/rhn,rnk->rhk/dot_general | solution.py:83
  349.5 13.7 %reduce-scatter.5.cloned.1.call-done = f32[16,64,512]{2,1,0:T(8,128)} async-done(((f32[16,128,512]{2,1,0:T(8,128)}), f32[16,64,512]{2,1,0:T(8,128)}) %reduce-scatter.5.cloned.1.call-update) | async-done | bytes 2097168 | tf_op jit(solution)/shard_map/reduce_scatter | solution.py:97
  363.2 1.8 divide_convert_fusion
  365.0 5.1 %fusion.5 = bf16[64,2,8,128]{3,2,1,0:T(8,128)(2,1)S(1)} fusion(bf16[64,512,128]{2,1,0:T(8,128)(2,1)} %param.17, bf16[16,64,512]{2,1,0:T(8,128)(2,1)S(1)} %divide_convert_fusion), kind=kOutput, calls=%fused_computation.21 | convolution fusion | flops 134348800 | bytes 9699328 | tf_op jit(solution)/shard_map/wyc,yca->wya/dot_general | solution.py:101
  (53 shorter events, 10.6 us)
Async XLA Ops:
  6.5 79.4 %copy-start = (bf16[16,128,512]{2,1,0:T(8,128)(2,1)S(1)}, bf16[16,128,512]{2,1,0:T(8,128)(2,1)}, u32[]{:S(2)}) copy-start(bf16[16,128,512]{2,1,0:T(8,128)(2,1)} %param.9) | copy-start | bytes 6291460
  6.5 30.3 %copy-start.1 = (bf16[48,2048]{1,0:T(8,128)(2,1)S(1)}, bf16[48,2048]{1,0:T(8,128)(2,1)}, u32[]{:S(2)}) copy-start(bf16[48,2048]{1,0:T(8,128)(2,1)} %param.13) | copy-start | bytes 589828
  42.5 33.9 %all-to-all-start.2 = ((bf16[8,40,2048]{2,1,0:T(8,128)(2,1)}), bf16[8,40,2048]{2,1,0:T(8,128)(2,1)S(1)}, u32[]{:S(2)}, u32[]{:S(2)}) async-start(bf16[8,40,2048]{2,1,0:T(8,128)(2,1)} %broadcast_select_fusion.1), calls=%async_computation.2 | async-start | bytes 2621440 | tf_op jit(solution)/shard_map/all_to_all | solution.py:48
  68.1 16.3 %copy-start.5 = (bf16[16,576]{1,0:T(8,128)(2,1)S(1)}, bf16[16,576]{1,0:T(8,128)(2,1)}, u32[]{:S(2)}) copy-start(bf16[16,576]{1,0:T(8,128)(2,1)} %param.11) | copy-start | bytes 55300
  68.2 16.3 %copy-start.6 = (s32[16]{0:T(128)S(1)}, s32[16]{0:T(128)}, u32[]{:S(2)}) copy-start(s32[16]{0:T(128)} %param.16) | copy-start | bytes 196
  76.4 231.7 %all-to-all-start.1 = ((bf16[8,40,32,512]{3,2,1,0:T(8,128)(2,1)}), bf16[8,40,32,512]{3,2,1,0:T(8,128)(2,1)}, u32[]{:S(2)}, u32[]{:S(2)}) async-start(bf16[8,40,32,512]{3,2,1,0:T(8,128)(2,1)} %broadcast_select_fusion), calls=%async_computation.1 | async-start | bytes 20971520 | tf_op jit(solution)/shard_map/all_to_all | solution.py:47
  81.6 267.1 %reduce-scatter.7.cloned.1.call-start = ((), (), s32[]{:S(2)}) async-start(), calls=%async_computation.6 | async-start | bytes 98304
  325.4 3.7 copy-start.2
  325.4 3.7 copy-start.3
  325.4 3.7 copy-start.4
  340.9 22.2 %reduce-scatter.5.cloned.1.call-start = ((), (), s32[]{:S(2)}) async-start(), calls=%async_computation.5 | async-start | bytes 6291456 | tf_op jit(solution)/shard_map/reduce_scatter | solution.py:97
Sparse Core Ops, SparseCore 0:
  341.0 6.5 reduce-scatter.6
  350.0 13.1 reduce-scatter.4
where the time goes:
time: 379 us; the launch traced here: 378 us
  waiting for transfers between devices  237 us (63%)
  local copies, waits for them, and re-layouts  55.2 us (15%)
  other arithmetic  25 us (7%)
  matrix products  22 us (6%)
  blocking collectives  16.1 us (4%)
  between operations  13.6 us (4%)
  starting transfers between devices  8.99 us (2%)
    all_to_all x1, waiting for transfers between devices, local(): lax.all_to_all(send_latent, 'dp', split_axis=0, concat_axis=0, tiled=True)  215 us
    reduce_scatter x1, waiting for transfers between devices, local(): lax.psum_scatter(numerator * factor[:, :, None], 'tp', scatter_dimension=...  13.7 us
    all_to_all x1, blocking collectives, local(): lax.all_to_all(wanted, 'dp', split_axis=0, concat_axis=0, tiled=True)  13.6 us
    gather x1, local copies, waits for them, and re-layouts, local(): jnp.take(got_latent.reshape(rank_count * capacity, run_len, latent_dim),...  12.6 us
    gather x1, local copies, waits for them, and re-layouts, local(): send_latent = jnp.take(cache_latent, asked_slots, axis=0)  12 us
    scatter x1, local copies, waits for them, and re-layouts, local(): jnp.zeros((rank_count, capacity), jnp.int32).at[src_flat, places]  11.2 us
    select_n x2, other arithmetic, local(): send_latent = jnp.take(cache_latent, asked_slots, axis=0)  10.1 us
    all_to_all x1, waiting for transfers between devices, local(): lax.all_to_all(send_rope, 'dp', split_axis=0, concat_axis=0, tiled=True)  8.25 us
  transfers between devices with their start and end apart: 4, of which 3 were waited for; matrix products, arithmetic and copies ran while one was open for 11% of the time, Pallas kernels for 0%

commit v1 on v0

--- a/solution.py
+++ b/solution.py
@@ -1,6 +1,10 @@
+import functools
+
 import jax
 import jax.numpy as jnp
 from jax import lax
+from jax.experimental import pallas as pl
+from jax.experimental.pallas import tpu as pltpu
 from jax.sharding import PartitionSpec as P
 
 softmax_scale = 192.0 ** (-0.5)
@@ -15,7 +19,7 @@
     return jnp.sum(before * onehot, axis=1)
 
 
-def local(
+def spread_local(
     q_latent,
     q_rope,
     new_entry,
@@ -104,6 +108,364 @@
     return value_projected_output.reshape(requests, -1).astype(jnp.bfloat16)
 
 
+MESH = pl.DeviceIdType.MESH
+up, down, across = 0, 1, 2
+chunk_count = 12
+vmem_pool_limit = 24 * 1024 * 1024
+
+
+def dot_nt(a, b):
+    return lax.dot_general(a, b, (((1,), (1,)), ((), ())), preferred_element_type=jnp.float32)
+
+
+def fused_kernel(
+    depth,
+    width,
+    early,
+    table,
+    lengths,
+    latent_hbm,
+    rope_hbm,
+    q_hbm,
+    value_hbm,
+    q_rope,
+    fresh,
+    out,
+    latent,
+    rope,
+    q_latent,
+    value,
+    keys,
+    rope_keys,
+    part,
+    other,
+    merged,
+    local_sem,
+    send_sem,
+    recv_sem,
+    pair_send,
+    pair_recv,
+):
+    me = lax.axis_index("dp")
+    lane = lax.axis_index("tp")
+    z, y = me // width, me % width
+    slots = latent_hbm.shape[0]
+    run_len = latent_hbm.shape[1]
+    latent_dim = latent_hbm.shape[2]
+    requests, heads = q_hbm.shape[0], q_hbm.shape[1]
+    rope_dim = q_rope.shape[2]
+    max_blocks = table.shape[0] // requests
+    half = run_len // 2
+    own_heads = heads // 2
+    chunk = slots // chunk_count
+    has_up, has_down = z + 1 < depth, z > 0
+
+    own = pl.ds(me * slots, slots)
+    local_copies = [
+        pltpu.make_async_copy(latent_hbm, latent.at[own], local_sem.at[0]),
+        pltpu.make_async_copy(rope_hbm, rope.at[own], local_sem.at[1]),
+        pltpu.make_async_copy(q_hbm, q_latent, local_sem.at[2]),
+        pltpu.make_async_copy(value_hbm, value, local_sem.at[3]),
+    ]
+    local_copies[0].start()
+    local_copies[1].start()
+
+    barrier = pltpu.get_barrier_semaphore()
+
+    def greet(target):
+        pl.semaphore_signal(barrier, inc=1, device_id=target, device_id_type=MESH)
+
+    greet({"tp": 1 - lane})
+    pl.when(has_up)(lambda: greet({"dp": me + width}))
+    pl.when(has_down)(lambda: greet({"dp": me - width}))
+    neighbours = 1 + has_up.astype(jnp.int32) + has_down.astype(jnp.int32)
+    if width == 2:
+        greet({"dp": z * width + 1 - y})
+        neighbours = neighbours + 1
+    pl.semaphore_wait(barrier, neighbours)
+    local_copies[0].wait()
+    local_copies[1].wait()
+
+    def piece(origin, c, way):
+        target = {up: me + width, down: me - width, across: z * width + 1 - y}[way]
+        rows = pl.ds(origin * slots + c * chunk, chunk)
+        return [
+            pltpu.make_async_remote_copy(
+                src_ref=array.at[rows],
+                dst_ref=array.at[rows],
+                send_sem=send_sem.at[n, way, origin, c],
+                recv_sem=recv_sem.at[n, origin, c],
+                device_id={"dp": target},
+                device_id_type=MESH,
+            )
+            for n, array in enumerate((latent, rope))
+        ]
+
+    def send(origin, c, way):
+        for copy in piece(origin, c, way):
+            copy.start()
+
+    def arrive(origin, c):
+        for copy in piece(origin, c, up):
+            copy.wait_recv()
+
+    def sent(origin, c, way):
+        for copy in piece(origin, c, way):
+            copy.wait_send()
+
+    def over(first, last, body):
+        def step(c, carry):
+            body(c)
+            return carry
+
+        lax.fori_loop(first, last, step, 0)
+
+    late = (early, chunk_count)
+
+    def own_first(c):
+        pl.when(has_up)(lambda: send(me, c, up))
+        pl.when(has_down)(lambda: send(me, c, down))
+        if width == 2:
+            send(me, c, across)
+
+    if width == 2:
+        over(0, early, lambda c: send(me, c, across))
+    over(*late, own_first)
+    local_copies[2].start()
+    local_copies[3].start()
+
+    def pass_on(t, columns, first, last, cross):
+        def body(c):
+            for column in columns:
+
+                @pl.when(z >= t)
+                def _():
+                    origin = (z - t) * width + column
+                    arrive(origin, c)
+                    pl.when(has_up)(lambda: send(origin, c, up))
+                    if cross:
+                        send(origin, c, across)
+
+                @pl.when(z + t < depth)
+                def _():
+                    origin = (z + t) * width + column
+                    arrive(origin, c)
+                    pl.when(has_down)(lambda: send(origin, c, down))
+                    if cross:
+                        send(origin, c, across)
+
+        over(first, last, body)
+
+    for t in range(1, depth):
+        pass_on(t, (y,), *late, width == 2)
+
+    if early:
+
+        def own_last(c):
+            partner = z * width + 1 - y
+            arrive(partner, c)
+            for origin in (me, partner):
+                pl.when(has_up)(lambda: send(origin, c, up))
+                pl.when(has_down)(lambda: send(origin, c, down))
+
+        over(0, early, own_last)
+        for t in range(1, depth):
+            pass_on(t, (0, 1), 0, early, False)
+
+    if width == 2:
+        order = [(z + t) % depth for t in range(depth)]
+        for place in order:
+            over(*late, lambda c: arrive(place * width + 1 - y, c))
+
+    local_copies[2].wait()
+    local_copies[3].wait()
+
+    def pair_copy(r):
+        return pltpu.make_async_remote_copy(
+            src_ref=part.at[r, pl.ds((1 - lane) * own_heads, own_heads)],
+            dst_ref=other.at[r],
+            send_sem=pair_send.at[r],
+            recv_sem=pair_recv.at[r],
+            device_id={"tp": 1 - lane},
+            device_id_type=MESH,
+        )
+
+    count = max_blocks * run_len
+    spot = lax.broadcasted_iota(jnp.int32, (heads, count), 1)
+    in_half = spot % (count // 2)
+    positions = (
+        in_half // half * (2 * run_len) + lane * run_len + spot // (count // 2) * half + in_half % half
+    )
+    is_first = lane == 0
+    stat_lane = lax.broadcasted_iota(jnp.int32, (heads, 128), 1)
+
+    def attend(r, carry):
+        side = r % 2
+        pl.when(r > 0)(lambda: pair_copy(r - 1).start())
+        for j in range(max_blocks):
+            block = table[r * max_blocks + j]
+            low = pl.ds(j * half, half)
+            keys[side, low, :] = latent[block, 0:half, :]
+            keys[side, pl.ds(count // 2 + j * half, half), :] = latent[block, half:run_len, :]
+            rope_keys[side, low, :] = rope[block]
+        q = q_latent[r]
+        q_rot = q_rope[r]
+        zero = jnp.zeros_like(q_rot)
+        rot = rope_keys[side]
+        all_keys = keys[side]
+        scores = dot_nt(q, all_keys)
+        low_scores = dot_nt(jnp.concatenate([q_rot, zero], axis=1), rot)
+        high_scores = dot_nt(jnp.concatenate([zero, q_rot], axis=1), rot)
+        scores = (scores + jnp.concatenate([low_scores, high_scores], axis=1)) * softmax_scale
+        new = fresh[pl.ds(r, 1), :]
+        new_latent = new[:, :latent_dim]
+        new_score = jnp.sum(q.astype(jnp.float32) * new_latent, axis=1, keepdims=True)
+        new_score = new_score + jnp.sum(
+            q_rot.astype(jnp.float32) * new[:, latent_dim : latent_dim + rope_dim], axis=1, keepdims=True
+        )
+        new_score = new_score * softmax_scale
+        in_range = positions < lengths[r]
+        top = jnp.max(jnp.where(in_range, scores, neg_fill), axis=1, keepdims=True)
+        top = jnp.where(is_first, jnp.maximum(top, new_score), top)
+        expo = jnp.where(in_range, jnp.exp(scores - top), 0.0)
+        weight = jnp.where(is_first, jnp.exp(new_score - top), 0.0)
+        den = jnp.sum(expo, axis=1, keepdims=True) + weight
+        num = jnp.dot(expo.astype(jnp.bfloat16), all_keys, preferred_element_type=jnp.float32)
+        num = num + weight.astype(jnp.bfloat16).astype(jnp.float32) * new_latent
+        part[r, :, 0:latent_dim] = num
+        part[r, :, latent_dim : latent_dim + 128] = jnp.where(stat_lane < 64, top, den)
+        return carry
+
+    lax.fori_loop(0, requests, attend, 0)
+    pair_copy(requests - 1).start()
+
+    def merge(r, carry):
+        pair_copy(r).wait_recv()
+        a = part[r, pl.ds(pl.multiple_of(lane * own_heads, own_heads), own_heads), :]
+        b = other[r]
+        top_a, top_b = a[:, latent_dim : latent_dim + 1], b[:, latent_dim : latent_dim + 1]
+        den_a, den_b = a[:, latent_dim + 64 : latent_dim + 65], b[:, latent_dim + 64 : latent_dim + 65]
+        top = jnp.maximum(top_a, top_b)
+        f_a, f_b = jnp.exp(top_a - top), jnp.exp(top_b - top)
+        total = a[:, :latent_dim] * f_a + b[:, :latent_dim] * f_b
+        merged[r] = total / (den_a * f_a + den_b * f_b)
+        return carry
+
+    lax.fori_loop(0, requests, merge, 0)
+
+    value_dim = value.shape[2]
+
+    def project(h, carry):
+        rows = merged[:, pl.ds(h, 1), :].reshape(requests, latent_dim).astype(jnp.bfloat16)
+        done = jnp.dot(rows, value[h], preferred_element_type=jnp.float32)
+        out[:, pl.ds(pl.multiple_of(h * value_dim, value_dim), value_dim)] = done.astype(out.dtype)
+        return carry
+
+    lax.fori_loop(0, own_heads, project, 0)
+
+    for place in range(depth):
+        mine = place * width + y
+
+        @pl.when(jnp.logical_and(place <= z, has_up))
+        def _():
+            over(*late, lambda c: sent(mine, c, up))
+            for column in range(width) if early else ():
+                over(0, early, lambda c: sent(place * width + column, c, up))
+
+        @pl.when(jnp.logical_and(place >= z, has_down))
+        def _():
+            over(*late, lambda c: sent(mine, c, down))
+            for column in range(width) if early else ():
+                over(0, early, lambda c: sent(place * width + column, c, down))
+
+        if width == 2:
+            over(*late, lambda c: sent(mine, c, across))
+    if early:
+        over(0, early, lambda c: sent(me, c, across))
+
+    def finish(r, carry):
+        pair_copy(r).wait_send()
+        return carry
+
+    lax.fori_loop(0, requests, finish, 0)
+
+
+def fused_local(
+    q_latent,
+    q_rope,
+    new_entry,
+    cache_latent,
+    cache_rope,
+    source_rank,
+    slot_index,
+    lengths,
+    value_up_weight,
+):
+    rank_count = lax.axis_size("dp")
+    width = 2 if rank_count % 2 == 0 else 1
+    depth = rank_count // width
+    early = chunk_count // 6 if width == 2 else 0
+    requests, max_blocks = slot_index.shape
+    slots, run_len, latent_dim = cache_latent.shape
+    heads = q_latent.shape[1]
+    rope_dim = q_rope.shape[1] // heads
+    own_heads, _, value_dim = value_up_weight.shape
+    half = run_len // 2
+    table = (source_rank.reshape(requests, max_blocks) * slots + slot_index).reshape(-1)
+    rope_pairs = (
+        cache_rope.reshape(slots, 2, half, rope_dim)
+        .transpose(0, 2, 1, 3)
+        .reshape(slots, half, 2 * rope_dim)
+    )
+    count = max_blocks * run_len
+    bf16, f32 = jnp.bfloat16, jnp.float32
+    smem = pl.BlockSpec(memory_space=pltpu.SMEM)
+    vmem = pl.BlockSpec(memory_space=pltpu.VMEM)
+    anywhere = pl.BlockSpec(memory_space=pl.ANY)
+    return pl.pallas_call(
+        functools.partial(fused_kernel, depth, width, early),
+        out_shape=jax.ShapeDtypeStruct((requests, own_heads * value_dim), bf16),
+        in_specs=[smem, smem, anywhere, anywhere, anywhere, anywhere, vmem, vmem],
+        out_specs=vmem,
+        scratch_shapes=[
+            pltpu.VMEM((rank_count * slots, run_len, latent_dim), bf16),
+            pltpu.VMEM((rank_count * slots, half, 2 * rope_dim), bf16),
+            pltpu.VMEM((requests, heads, latent_dim), bf16),
+            pltpu.VMEM(value_up_weight.shape, bf16),
+            pltpu.VMEM((2, count, latent_dim), bf16),
+            pltpu.VMEM((2, count // 2, 2 * rope_dim), bf16),
+            pltpu.VMEM((requests, heads, latent_dim + 128), f32),
+            pltpu.VMEM((requests, own_heads, latent_dim + 128), f32),
+            pltpu.VMEM((requests, own_heads, latent_dim), f32),
+            pltpu.SemaphoreType.DMA((4,)),
+            pltpu.SemaphoreType.DMA((2, 3, rank_count, chunk_count)),
+            pltpu.SemaphoreType.DMA((2, rank_count, chunk_count)),
+            pltpu.SemaphoreType.DMA((requests,)),
+            pltpu.SemaphoreType.DMA((requests,)),
+        ],
+        compiler_params=pltpu.CompilerParams(
+            collective_id=0, has_side_effects=True, vmem_limit_bytes=60 * 1024 * 1024
+        ),
+    )(
+        table,
+        lengths,
+        cache_latent,
+        rope_pairs,
+        q_latent,
+        value_up_weight,
+        q_rope.reshape(requests, heads, rope_dim),
+        new_entry.astype(f32),
+    )
+
+
+def local(*args):
+    cache_latent = args[3]
+    pool_bytes = lax.axis_size("dp") * cache_latent.size * 2
+    fits = pool_bytes <= vmem_pool_limit and lax.axis_size("tp") == 2
+    fits = fits and cache_latent.shape[0] % chunk_count == 0
+    return (fused_local if fits else spread_local)(*args)
+
+
 def solution(mesh):
     placed = (
         P(("pop", "dp"), None, None),

time: 379 us -> 180 us (0.47)
  waiting for transfers between devices: 237 us -> 0 us
  Pallas kernels: 0 us -> 171 us
  local copies, waits for them, and re-layouts: 55.2 us -> 6.14 us
  other arithmetic: 25 us -> 2.1 us
  matrix products: 22 us -> 0 us
  blocking collectives: 16.1 us -> 0 us
  between operations: 13.6 us -> 0.02 us
  starting transfers between devices: 8.99 us -> 0 us
    all_to_all x2 -> x0, waiting for transfers between devices: 223 us -> none  [the longest x1 215 us: local(): lax.all_to_all(send_latent, 'dp', split_axis=0, concat_axis=0, tiled=True)]
    pallas_call x0 -> x1, Pallas kernels: none -> 171 us  [fused_local(): pl.pallas_call(functools.partial(fused_kernel, depth, width, early), out_...]
    gather x5 -> x0, local copies, waits for them, and re-layouts: 34.4 us -> none  [the longest x1 12.6 us: local(): jnp.take(got_latent.reshape(rank_count * capacity, run_len, latent_dim),...]
    dot_general x6 -> x0, matrix products: 22 us -> none  [the longest x1 7.64 us: local(): jnp.einsum('rhn,rnk->rhk', expo.astype(jnp.bfloat16), keys_latent, prefer...]
    select_n x6 -> x0, other arithmetic: 17.4 us -> none  [the longest x2 10.1 us: local(): send_latent = jnp.take(cache_latent, asked_slots, axis=0)]
    reduce_scatter x1 -> x0, waiting for transfers between devices: 13.7 us -> none  [local(): lax.psum_scatter(numerator * factor[:, :, None], 'tp', scatter_dimension=...]
    all_to_all x1 -> x0, blocking collectives: 13.6 us -> none  [local(): lax.all_to_all(wanted, 'dp', split_axis=0, concat_axis=0, tiled=True)]
    scatter x1 -> x0, local copies, waits for them, and re-layouts: 11.2 us -> none  [local(): jnp.zeros((rank_count, capacity), jnp.int32).at[src_flat, places]]
  transfers between devices with their start and end apart: 4 -> 0, of which waited for: 3 -> 0; matrix products, arithmetic and copies ran while one was open for 11% -> 0% of each run, Pallas kernels for 0% -> 0%
where the time goes in v1:
time: 180 us
  Pallas kernels  171 us (95%)
  local copies, waits for them, and re-layouts  6.14 us (3%)
  other arithmetic  2.1 us (1%)
    pallas_call x1, Pallas kernels, fused_local(): pl.pallas_call(functools.partial(fused_kernel, depth, width, early), out_...  171 us

profile of v1, /device:TPU:0, one launch (start us, length us, event | category | flops | bytes accessed | tf_op | source)
XLA Modules:
  0.0 179.7 jit_solution(8726507290092861598)
XLA Ops:
  0.0 0.0 copy-start
  0.0 0.8 bitcast_add_fusion
  0.8 0.6 reshape.15.table
  1.4 1.3 convert_element_type.3.fresh
  2.7 1.3 reshape.16
  4.1 0.3 copy.15
  4.4 0.9 reshape.17.rope_hbm
  5.3 0.0 copy-done
  5.3 1.3 reshape.18.q_rope
  6.6 171.5 %shard_map.91 = bf16[16,8192]{1,0:T(8,128)(2,1)} custom-call(s32[256]{0:T(256)} %reshape.15.table, s32[16]{0:T(128)} %lengths.1, bf16[48,32,512]{2,1,0:T(8,128)(2,1)} %latent_hbm.1, bf16[48,16,128]{2,1,0:T(8,128)(2,1)} %reshape.17.rope_hbm, bf16[16,128,512]{2,1,0:T(8,128)(2,1)} %q_hbm.1, bf16[64,512,128]{2,1,0:T(8,128)(2,1)} %value_hbm.1, ...), custom_call_target="tpu_custom_call" | custom-call | tf_op jit(solution)/shard_map/pallas_call | solution.py:425
  178.1 1.7 copy.17
Async XLA Ops:
  0.0 5.3 %copy-start = (bf16[16,8192]{1,0:T(8,128)(2,1)S(1)}, bf16[16,8192]{1,0:T(8,128)(2,1)}, u32[]{:S(2)}) copy-start(bf16[16,8192]{1,0:T(8,128)(2,1)} %param.10) | copy-start | bytes 786436

commit v2 on v1

--- a/solution.py
+++ b/solution.py
@@ -110,7 +110,7 @@
 
 MESH = pl.DeviceIdType.MESH
 up, down, across = 0, 1, 2
-chunk_count = 12
+chunk_count = 6
 vmem_pool_limit = 24 * 1024 * 1024
 
 
@@ -122,14 +122,15 @@
     depth,
     width,
     early,
-    table,
+    sources,
+    slot_table,
     lengths,
     latent_hbm,
     rope_hbm,
     q_hbm,
     value_hbm,
     q_rope,
-    fresh,
+    new_entry,
     out,
     latent,
     rope,
@@ -140,6 +141,9 @@
     part,
     other,
     merged,
+    q_low,
+    q_high,
+    fresh,
     local_sem,
     send_sem,
     recv_sem,
@@ -153,8 +157,8 @@
     run_len = latent_hbm.shape[1]
     latent_dim = latent_hbm.shape[2]
     requests, heads = q_hbm.shape[0], q_hbm.shape[1]
-    rope_dim = q_rope.shape[2]
-    max_blocks = table.shape[0] // requests
+    rope_dim = q_rope.shape[1] // heads
+    max_blocks = slot_table.shape[1]
     half = run_len // 2
     own_heads = heads // 2
     chunk = slots // chunk_count
@@ -186,73 +190,93 @@
     local_copies[0].wait()
     local_copies[1].wait()
 
-    def piece(origin, c, way):
+    def piece(n, origin, c, way):
         target = {up: me + width, down: me - width, across: z * width + 1 - y}[way]
-        rows = pl.ds(origin * slots + c * chunk, chunk)
-        return [
-            pltpu.make_async_remote_copy(
-                src_ref=array.at[rows],
-                dst_ref=array.at[rows],
-                send_sem=send_sem.at[n, way, origin, c],
-                recv_sem=recv_sem.at[n, origin, c],
-                device_id={"dp": target},
-                device_id_type=MESH,
-            )
-            for n, array in enumerate((latent, rope))
-        ]
-
-    def send(origin, c, way):
-        for copy in piece(origin, c, way):
-            copy.start()
-
-    def arrive(origin, c):
-        for copy in piece(origin, c, up):
-            copy.wait_recv()
-
-    def sent(origin, c, way):
-        for copy in piece(origin, c, way):
-            copy.wait_send()
+        array = (latent, rope)[n]
+        if n == 0:
+            rows = pl.ds(origin * slots + c * chunk, chunk)
+        elif c == 0:
+            rows = pl.ds(origin * slots, early * chunk)
+        else:
+            rows = pl.ds(origin * slots + early * chunk, slots - early * chunk)
+        return pltpu.make_async_remote_copy(
+            src_ref=array.at[rows],
+            dst_ref=array.at[rows],
+            send_sem=send_sem.at[way, origin, c + n * chunk_count],
+            recv_sem=recv_sem.at[origin, c + n * chunk_count],
+            device_id={"dp": target},
+            device_id_type=MESH,
+        )
+
+    def send(n, origin, c, way):
+        piece(n, origin, c, way).start()
+
+    def arrive(n, origin, c):
+        piece(n, origin, c, up).wait_recv()
+
+    def sent(n, origin, c, way):
+        piece(n, origin, c, way).wait_send()
 
     def over(first, last, body):
         def step(c, carry):
-            body(c)
+            body(0, c)
             return carry
 
         lax.fori_loop(first, last, step, 0)
+        body(1, 0 if first == 0 and early else 1)
 
     late = (early, chunk_count)
 
-    def own_first(c):
-        pl.when(has_up)(lambda: send(me, c, up))
-        pl.when(has_down)(lambda: send(me, c, down))
+    def own_first(n, c):
+        pl.when(has_up)(lambda: send(n, me, c, up))
+        pl.when(has_down)(lambda: send(n, me, c, down))
         if width == 2:
-            send(me, c, across)
+            send(n, me, c, across)
 
     if width == 2:
-        over(0, early, lambda c: send(me, c, across))
+        over(0, early, lambda n, c: send(n, me, c, across))
     over(*late, own_first)
     local_copies[2].start()
     local_copies[3].start()
 
+    first_half = lax.broadcasted_iota(jnp.int32, (requests, 128), 1) < rope_dim
+
+    def spread(p, carry):
+        x = q_rope[:, pl.ds(pl.multiple_of(p * 128, 128), 128)].astype(jnp.float32)
+        turned = pltpu.roll(x, rope_dim, 1)
+
+        def put(array, head, values):
+            array[:, pl.ds(head, 1), :] = values.reshape(requests, 1, 128)
+
+        put(q_low, 2 * p, jnp.where(first_half, x, 0.0))
+        put(q_high, 2 * p, jnp.where(first_half, 0.0, turned))
+        put(q_low, 2 * p + 1, jnp.where(first_half, turned, 0.0))
+        put(q_high, 2 * p + 1, jnp.where(first_half, 0.0, x))
+        return carry
+
+    lax.fori_loop(0, heads // 2, spread, 0)
+    fresh[...] = jnp.zeros_like(fresh)
+    fresh[:, 0 : latent_dim + rope_dim] = new_entry[...].astype(jnp.float32)
+
     def pass_on(t, columns, first, last, cross):
-        def body(c):
+        def body(n, c):
             for column in columns:
 
                 @pl.when(z >= t)
                 def _():
                     origin = (z - t) * width + column
-                    arrive(origin, c)
-                    pl.when(has_up)(lambda: send(origin, c, up))
+                    arrive(n, origin, c)
+                    pl.when(has_up)(lambda: send(n, origin, c, up))
                     if cross:
-                        send(origin, c, across)
+                        send(n, origin, c, across)
 
                 @pl.when(z + t < depth)
                 def _():
                     origin = (z + t) * width + column
-                    arrive(origin, c)
-                    pl.when(has_down)(lambda: send(origin, c, down))
+                    arrive(n, origin, c)
+                    pl.when(has_down)(lambda: send(n, origin, c, down))
                     if cross:
-                        send(origin, c, across)
+                        send(n, origin, c, across)
 
         over(first, last, body)
 
@@ -261,12 +285,12 @@
 
     if early:
 
-        def own_last(c):
+        def own_last(n, c):
             partner = z * width + 1 - y
-            arrive(partner, c)
+            arrive(n, partner, c)
             for origin in (me, partner):
-                pl.when(has_up)(lambda: send(origin, c, up))
-                pl.when(has_down)(lambda: send(origin, c, down))
+                pl.when(has_up)(lambda: send(n, origin, c, up))
+                pl.when(has_down)(lambda: send(n, origin, c, down))
 
         over(0, early, own_last)
         for t in range(1, depth):
@@ -275,7 +299,7 @@
     if width == 2:
         order = [(z + t) % depth for t in range(depth)]
         for place in order:
-            over(*late, lambda c: arrive(place * width + 1 - y, c))
+            over(*late, lambda n, c: arrive(n, place * width + 1 - y, c))
 
     local_copies[2].wait()
     local_copies[3].wait()
@@ -303,25 +327,24 @@
         side = r % 2
         pl.when(r > 0)(lambda: pair_copy(r - 1).start())
         for j in range(max_blocks):
-            block = table[r * max_blocks + j]
+            block = sources[r, j] * slots + slot_table[r, j]
             low = pl.ds(j * half, half)
             keys[side, low, :] = latent[block, 0:half, :]
             keys[side, pl.ds(count // 2 + j * half, half), :] = latent[block, half:run_len, :]
             rope_keys[side, low, :] = rope[block]
         q = q_latent[r]
-        q_rot = q_rope[r]
-        zero = jnp.zeros_like(q_rot)
+        q_rot = q_low[r]
         rot = rope_keys[side]
         all_keys = keys[side]
         scores = dot_nt(q, all_keys)
-        low_scores = dot_nt(jnp.concatenate([q_rot, zero], axis=1), rot)
-        high_scores = dot_nt(jnp.concatenate([zero, q_rot], axis=1), rot)
+        low_scores = dot_nt(q_rot.astype(jnp.bfloat16), rot)
+        high_scores = dot_nt(q_high[r].astype(jnp.bfloat16), rot)
         scores = (scores + jnp.concatenate([low_scores, high_scores], axis=1)) * softmax_scale
         new = fresh[pl.ds(r, 1), :]
         new_latent = new[:, :latent_dim]
         new_score = jnp.sum(q.astype(jnp.float32) * new_latent, axis=1, keepdims=True)
         new_score = new_score + jnp.sum(
-            q_rot.astype(jnp.float32) * new[:, latent_dim : latent_dim + rope_dim], axis=1, keepdims=True
+            q_rot * new[:, latent_dim : latent_dim + 128], axis=1, keepdims=True
         )
         new_score = new_score * softmax_scale
         in_range = positions < lengths[r]
@@ -336,7 +359,7 @@
         part[r, :, latent_dim : latent_dim + 128] = jnp.where(stat_lane < 64, top, den)
         return carry
 
-    lax.fori_loop(0, requests, attend, 0)
+    lax.fori_loop(0, requests, attend, 0, unroll=2)
     pair_copy(requests - 1).start()
 
     def merge(r, carry):
@@ -351,7 +374,7 @@
         merged[r] = total / (den_a * f_a + den_b * f_b)
         return carry
 
-    lax.fori_loop(0, requests, merge, 0)
+    lax.fori_loop(0, requests, merge, 0, unroll=2)
 
     value_dim = value.shape[2]
 
@@ -361,27 +384,27 @@
         out[:, pl.ds(pl.multiple_of(h * value_dim, value_dim), value_dim)] = done.astype(out.dtype)
         return carry
 
-    lax.fori_loop(0, own_heads, project, 0)
+    lax.fori_loop(0, own_heads, project, 0, unroll=8)
 
     for place in range(depth):
         mine = place * width + y
 
         @pl.when(jnp.logical_and(place <= z, has_up))
         def _():
-            over(*late, lambda c: sent(mine, c, up))
+            over(*late, lambda n, c: sent(n, mine, c, up))
             for column in range(width) if early else ():
-                over(0, early, lambda c: sent(place * width + column, c, up))
+                over(0, early, lambda n, c: sent(n, place * width + column, c, up))
 
         @pl.when(jnp.logical_and(place >= z, has_down))
         def _():
-            over(*late, lambda c: sent(mine, c, down))
+            over(*late, lambda n, c: sent(n, mine, c, down))
             for column in range(width) if early else ():
-                over(0, early, lambda c: sent(place * width + column, c, down))
+                over(0, early, lambda n, c: sent(n, place * width + column, c, down))
 
         if width == 2:
-            over(*late, lambda c: sent(mine, c, across))
+            over(*late, lambda n, c: sent(n, mine, c, across))
     if early:
-        over(0, early, lambda c: sent(me, c, across))
+        over(0, early, lambda n, c: sent(n, me, c, across))
 
     def finish(r, carry):
         pair_copy(r).wait_send()
@@ -411,7 +434,6 @@
     rope_dim = q_rope.shape[1] // heads
     own_heads, _, value_dim = value_up_weight.shape
     half = run_len // 2
-    table = (source_rank.reshape(requests, max_blocks) * slots + slot_index).reshape(-1)
     rope_pairs = (
         cache_rope.reshape(slots, 2, half, rope_dim)
         .transpose(0, 2, 1, 3)
@@ -425,7 +447,7 @@
     return pl.pallas_call(
         functools.partial(fused_kernel, depth, width, early),
         out_shape=jax.ShapeDtypeStruct((requests, own_heads * value_dim), bf16),
-        in_specs=[smem, smem, anywhere, anywhere, anywhere, anywhere, vmem, vmem],
+        in_specs=[smem, smem, smem, anywhere, anywhere, anywhere, anywhere, vmem, vmem],
         out_specs=vmem,
         scratch_shapes=[
             pltpu.VMEM((rank_count * slots, run_len, latent_dim), bf16),
@@ -437,9 +459,12 @@
             pltpu.VMEM((requests, heads, latent_dim + 128), f32),
             pltpu.VMEM((requests, own_heads, latent_dim + 128), f32),
             pltpu.VMEM((requests, own_heads, latent_dim), f32),
+            pltpu.VMEM((requests, heads, 128), f32),
+            pltpu.VMEM((requests, heads, 128), f32),
+            pltpu.VMEM((requests, latent_dim + 128), f32),
             pltpu.SemaphoreType.DMA((4,)),
-            pltpu.SemaphoreType.DMA((2, 3, rank_count, chunk_count)),
-            pltpu.SemaphoreType.DMA((2, rank_count, chunk_count)),
+            pltpu.SemaphoreType.DMA((3, rank_count, chunk_count + 2)),
+            pltpu.SemaphoreType.DMA((rank_count, chunk_count + 2)),
             pltpu.SemaphoreType.DMA((requests,)),
             pltpu.SemaphoreType.DMA((requests,)),
         ],
@@ -447,14 +472,15 @@
             collective_id=0, has_side_effects=True, vmem_limit_bytes=60 * 1024 * 1024
         ),
     )(
-        table,
+        source_rank.reshape(requests, max_blocks),
+        slot_index,
         lengths,
         cache_latent,
         rope_pairs,
         q_latent,
         value_up_weight,
-        q_rope.reshape(requests, heads, rope_dim),
-        new_entry.astype(f32),
+        q_rope,
+        new_entry,
     )
 
 
@@ -462,7 +488,7 @@
     cache_latent = args[3]
     pool_bytes = lax.axis_size("dp") * cache_latent.size * 2
     fits = pool_bytes <= vmem_pool_limit and lax.axis_size("tp") == 2
-    fits = fits and cache_latent.shape[0] % chunk_count == 0
+    fits = fits and cache_latent.shape[0] % chunk_count == 0 and args[1].shape[1] == args[0].shape[1] * 64
     return (fused_local if fits else spread_local)(*args)
 
 

time: 180 us -> 164 us (0.911)
  Pallas kernels: 171 us -> 159 us
  other arithmetic: 2.1 us -> 0 us
  local copies, waits for them, and re-layouts: 6.14 us -> 4.18 us
    pallas_call x1, Pallas kernels: 171 us -> 159 us  [fused_local(): pl.pallas_call(functools.partial(fused_kernel, depth, width, early), out_...]
    reshape x2 -> x0, local copies, waits for them, and re-layouts: 1.96 us -> none  [the longest x1 1.33 us: fused_local(): q_rope.reshape(requests, heads, rope_dim)]
where the time goes in v2:
time: 164 us
  Pallas kernels  159 us (97%)
  local copies, waits for them, and re-layouts  4.18 us (3%)
    pallas_call x1, Pallas kernels, fused_local(): pl.pallas_call(functools.partial(fused_kernel, depth, width, early), out_...  159 us

profile of v2, /device:TPU:0, one launch (start us, length us, event | category | flops | bytes accessed | tf_op | source)
XLA Modules:
  0.0 163.5 jit_solution(12029105199540419353)
XLA Ops:
  0.0 1.3 reshape.10
  1.3 0.3 copy.12
  1.6 0.9 reshape.11.rope_hbm
  2.5 159.3 %shard_map.91 = bf16[16,8192]{1,0:T(8,128)(2,1)} custom-call(s32[16,16]{1,0:T(8,128)} %bitcast.5, s32[16,16]{1,0:T(8,128)} %slot_table.1, s32[16]{0:T(128)} %lengths.1, bf16[48,32,512]{2,1,0:T(8,128)(2,1)} %latent_hbm.1, bf16[48,16,128]{2,1,0:T(8,128)(2,1)} %reshape.11.rope_hbm, bf16[16,128,512]{2,1,0:T(8,128)(2,1)} %q_hbm.1, ...), custom_call_target="tpu_custom_call" | custom-call | tf_op jit(solution)/shard_map/pallas_call | solution.py:447
  161.8 1.7 %copy.14 = bf16[16,8192]{1,0:T(8,128)(2,1)} copy(bf16[16,8192]{1,0:T(8,128)(2,1)} %shard_map.91) | data formatting | bytes 524288
